TPU v7x, 256 devices: a whole 4x4x8 slice. The times are simulated.
256 devices in a mesh: dp: 8 (over z), expert: 8 (over x, core), tensor: 4 (over y).
Axes of the slice: x: 4, y: 4, z: 8, core: 2. Of those that a mesh axis runs over, the one named last changes fastest.
Arguments:
- skip_stream_entry: bfloat16 [4096, 4096], P(('dp', 'expert', 'tensor')), may hold values from -6 to 6
- question_vectors: bfloat16 [4096, 2048], P(('dp', 'expert'), 'tensor'), may hold values from -5 to 5
- fresh_lookup_vectors: bfloat16 [4096, 512], P(('dp', 'expert'), 'tensor'), may hold values from -5 to 5
- fresh_content_vectors: bfloat16 [4096, 512], P(('dp', 'expert'), 'tensor'), may hold values from -10 to 10
- stored_lookup_sheets: bfloat16 [2560, 4, 128, 128], P(('dp', 'expert'), 'tensor'), may hold values from -5 to 5
- stored_content_sheets: bfloat16 [2560, 4, 128, 128], P(('dp', 'expert'), 'tensor'), may hold values from -10 to 10
- sequence_sheet_map: int32 [1088, 8], P(('dp', 'expert')), may hold values from 0 to 39
- stored_position_counts: int32 [1088], P(('dp', 'expert')), may hold values from 2 to 1024
- attention_merge_matrix: bfloat16 [2048, 4096], P('tensor'), may hold values from -0.59765625 to 0.59765625
- premix_scale_factor: bfloat16 [4096], replicated, may hold values from 0.5 to 1.5
- chosen_specialists: int32 [4096, 2], P(('dp', 'expert', 'tensor')), may hold values from 0 to 7, all different within a row; in each aligned block of 16 rows (0 to 15, 16 to 31, ...) at most 6 rows name the same one
- selection_shares: float32 [4096, 2], P(('dp', 'expert', 'tensor')), may hold values from 0.2 to 1
- allowed_placements: int32 [8], replicated, may hold values from 2 to 3
- favored_specialist: int32 [1], replicated, may hold values from 0 to 7
- gating_matrices: bfloat16 [8, 7168, 4096], P('expert', ('dp', 'tensor')), may hold values from -0.09375 to 0.09375
- expand_matrices: bfloat16 [8, 7168, 4096], P('expert', ('dp', 'tensor')), may hold values from -0.09375 to 0.09375
- contract_matrices: bfloat16 [8, 7168, 4096], P('expert', ('dp', 'tensor')), may hold values from -0.0625 to 0.0625
Outputs:
- layer_out: bfloat16 [4096, 4096], P(('dp', 'expert', 'tensor'))
Inputs may be any that keep to these rules, and one draw needn't show every extreme that they name: `chosen_specialists`: in the 16 rows of one device no expert is named by more than 6 rows; a token names two different experts.
All inputs are finite; a program needn't handle non-finite values.
Results may differ from a plain program's by a relative error of at most 0.018.
Values may be sent and summed in bfloat16 or wider, within the bound.
A program may use at most 128 MiB of HBM per device.

v0:
```python
from functools import reduce
import math
import jax
import jax.numpy as jnp
from jax import lax
from jax.sharding import PartitionSpec as P

HD = 128
PLACEMENT_MOST = 6


def normalize(parts):
    highest = reduce(
        jnp.maximum,
        [
            jnp.max(jnp.where(visible, scores, -jnp.inf), axis=-1, keepdims=True)
            for scores, visible in parts
        ],
    )
    portions = [jnp.where(visible, jnp.exp(scores - highest), 0.0) for scores, visible in parts]
    denominator = reduce(
        jnp.add, [jnp.sum(portion, axis=-1, keepdims=True) for portion in portions]
    )
    return [(portion / denominator).astype(jnp.bfloat16) for portion in portions]


def attend(question_vectors, new_keys, new_values, key_pages, value_pages, table, spans):
    rows_all, head_count, head_width = question_vectors.shape
    kv_heads = new_keys.shape[1]
    group_size = head_count // kv_heads
    single_count = spans.shape[0] - 1
    page_count = table.shape[1]
    page_width = key_pages.shape[2]
    context = page_count * page_width
    inverse_root = 1.0 / math.sqrt(head_width)
    page_keys = key_pages[table]
    page_values = value_pages[table]
    grouped = question_vectors.reshape(rows_all, kv_heads, group_size, head_width)
    positions = jnp.arange(context, dtype=jnp.int32)
    single_q = grouped[:single_count]
    cache_dec = (
        jnp.einsum(
            "rkgh,rmkph->rkgmp",
            single_q,
            page_keys[:single_count],
            preferred_element_type=jnp.float32,
        ).reshape(single_count, kv_heads, group_size, context)
        * inverse_root
    )
    seen_dec = (positions[None, :] < spans[:single_count, None])[:, None, None, :]
    own_dec = (
        jnp.einsum(
            "rkgh,rkh->rkg", single_q, new_keys[:single_count], preferred_element_type=jnp.float32
        )[..., None]
        * inverse_root
    )
    weight_cache, weight_own = normalize(
        [(cache_dec, seen_dec), (own_dec, jnp.full(own_dec.shape, True))]
    )
    out_dec = jnp.einsum(
        "rkgmp,rmkph->rkgh",
        weight_cache.reshape(single_count, kv_heads, group_size, page_count, page_width),
        page_values[:single_count],
        preferred_element_type=jnp.float32,
    )
    out_dec = (
        out_dec
        + weight_own.astype(jnp.float32)
        * new_values[:single_count].astype(jnp.float32)[:, :, None, :]
    )
    prompt_q = grouped[single_count:]
    prompt_rows = rows_all - single_count
    cache_pro = (
        jnp.einsum(
            "rkgh,mkph->rkgmp",
            prompt_q,
            page_keys[single_count],
            preferred_element_type=jnp.float32,
        ).reshape(prompt_rows, kv_heads, group_size, context)
        * inverse_root
    )
    seen_pro = (positions < spans[single_count])[None, None, None, :]
    new_pro = (
        jnp.einsum(
            "rkgh,mkh->rkgm", prompt_q, new_keys[single_count:], preferred_element_type=jnp.float32
        )
        * inverse_root
    )
    prompt_index = jnp.arange(prompt_rows, dtype=jnp.int32)
    causal = (prompt_index[:, None] >= prompt_index[None, :])[:, None, None, :]
    weight_cpro, weight_npro = normalize([(cache_pro, seen_pro), (new_pro, causal)])
    out_pro = jnp.einsum(
        "rkgmp,mkph->rkgh",
        weight_cpro.reshape(prompt_rows, kv_heads, group_size, page_count, page_width),
        page_values[single_count],
        preferred_element_type=jnp.float32,
    )
    out_pro = out_pro + jnp.einsum(
        "rkgm,mkh->rkgh", weight_npro, new_values[single_count:], preferred_element_type=jnp.float32
    )
    joined = jnp.concatenate([out_dec, out_pro], axis=0).astype(jnp.bfloat16)
    return joined.reshape(rows_all, head_count * head_width)


def slot_table(member, ranking, keeping, slot_count):
    slot_hit = (
        ranking[:, :, None, None] == jnp.arange(slot_count, dtype=jnp.int32)[None, None, None, :]
    )
    return ((member[..., None] > 0) & keeping[:, :, None, None] & slot_hit).astype(jnp.bfloat16)


def expert_pass(send, gating_matrices, expand_matrices, contract_matrices):
    specialist_index, slot_count, model_width = send.shape
    holders = lax.axis_size("expert")
    local_count = gating_matrices.shape[0]
    arrived = lax.all_to_all(
        send.reshape(holders, local_count, slot_count, model_width),
        "expert",
        split_axis=0,
        concat_axis=0,
        tiled=True,
    )
    row_piece = lax.all_gather(arrived, ("dp", "tensor"), axis=0, tiled=True)
    gate_part = jnp.einsum(
        "qesd,efd->qesf", row_piece, gating_matrices, preferred_element_type=jnp.float32
    )
    up_part = jnp.einsum(
        "qesd,efd->qesf", row_piece, expand_matrices, preferred_element_type=jnp.float32
    )
    hidden = (jax.nn.silu(gate_part) * up_part).astype(jnp.bfloat16)
    summed = lax.psum_scatter(
        jnp.einsum(
            "qesf,efd->qesd", hidden, contract_matrices, preferred_element_type=jnp.float32
        ).astype(jnp.bfloat16),
        ("dp", "tensor"),
        scatter_dimension=0,
        tiled=True,
    )
    arrived_back = lax.all_to_all(summed, "expert", split_axis=0, concat_axis=0, tiled=True)
    return arrived_back.reshape(specialist_index, slot_count, model_width)


def local(
    skip_stream_entry,
    question_vectors,
    fresh_lookup_vectors,
    fresh_content_vectors,
    stored_lookup_sheets,
    stored_content_sheets,
    sequence_sheet_map,
    stored_position_counts,
    attention_merge_matrix,
    premix_scale_factor,
    chosen_specialists,
    selection_shares,
    allowed_placements,
    favored_specialist,
    gating_matrices,
    expand_matrices,
    contract_matrices,
):
    token_count = chosen_specialists.shape[0]
    specialist_index = allowed_placements.shape[0]
    picked = (
        chosen_specialists[:, :, None]
        == jnp.arange(specialist_index, dtype=jnp.int32)[None, None, :]
    ).astype(jnp.int32)
    flat_routes = picked.reshape(token_count * 2, specialist_index)
    busiest_specialist = favored_specialist[0]
    before = (jnp.cumsum(flat_routes, axis=0) - flat_routes).reshape(
        token_count, 2, specialist_index
    )
    ranking = jnp.sum(before * picked, axis=2)
    placement_ceiling = jnp.where(
        jnp.arange(specialist_index, dtype=jnp.int32) == busiest_specialist,
        PLACEMENT_MOST,
        allowed_placements,
    )
    keeping = ranking < jnp.sum(picked * placement_ceiling[None, None, :], axis=2)
    row_total = question_vectors.shape[0]
    heads_out = attend(
        question_vectors.reshape(row_total, -1, HD),
        fresh_lookup_vectors.reshape(row_total, -1, HD),
        fresh_content_vectors.reshape(row_total, -1, HD),
        stored_lookup_sheets,
        stored_content_sheets,
        sequence_sheet_map,
        stored_position_counts,
    )
    own_attn = lax.psum_scatter(
        jnp.dot(heads_out, attention_merge_matrix, preferred_element_type=jnp.float32).astype(
            jnp.bfloat16
        ),
        "tensor",
        scatter_dimension=0,
        tiled=True,
    ).astype(jnp.float32)
    stream = (skip_stream_entry.astype(jnp.float32) + own_attn).astype(jnp.bfloat16)
    wide = stream.astype(jnp.float32)
    squares = jnp.mean(wide * wide, axis=1, keepdims=True)
    normed = (wide * lax.rsqrt(squares + 1e-05) * premix_scale_factor.astype(jnp.float32)).astype(
        jnp.bfloat16
    )
    main_slots = PLACEMENT_MOST
    table_main = slot_table(picked, ranking, keeping, main_slots)
    send = jnp.einsum(
        "nkes,nd->esd", table_main, normed, preferred_element_type=jnp.float32
    ).astype(jnp.bfloat16)
    expert_out = expert_pass(send, gating_matrices, expand_matrices, contract_matrices)
    chosen = jnp.einsum("nkes,esd->nkd", table_main, expert_out, preferred_element_type=jnp.float32)
    mixed = jnp.sum(selection_shares[:, :, None] * chosen, axis=1)
    return (wide + mixed).astype(jnp.bfloat16)


def solution(mesh):
    placed = (
        P(("dp", "expert", "tensor"), None),
        P(("dp", "expert"), "tensor"),
        P(("dp", "expert"), "tensor"),
        P(("dp", "expert"), "tensor"),
        P(("dp", "expert"), "tensor", None, None),
        P(("dp", "expert"), "tensor", None, None),
        P(("dp", "expert"), None),
        P(("dp", "expert")),
        P("tensor", None),
        P(),
        P(("dp", "expert", "tensor"), None),
        P(("dp", "expert", "tensor"), None),
        P(),
        P(),
        P("expert", ("dp", "tensor"), None),
        P("expert", ("dp", "tensor"), None),
        P("expert", ("dp", "tensor"), None),
    )
    return jax.shard_map(
        local,
        mesh=mesh,
        in_specs=placed,
        out_specs=P(("dp", "expert", "tensor"), None),
        check_vma=False,
    )
```

profile of v0, /device:TPU:1, one launch (start us, length us, event | category | flops | bytes accessed | tf_op | source)
XLA Modules:
  0.0 500.2 jit_solution(16697747358621664481)
XLA Ops:
  6.6 0.9 slice.44
  7.4 1.2 slice.49
  8.7 1.2 broadcast_compare_fusion.1
  9.8 0.7 compare_select_fusion
  10.5 1.3 slice_bitcast_fusion.5
  11.8 0.1 copy.32
  11.9 0.1 reshape.332
  12.0 1.3 slice_convert_fusion
  13.3 1.6 select_reduce_fusion.2
  14.8 8.8 %gather_fusion.1 = bf16[136,128,128]{2,1,0:T(8,128)(2,1)} fusion(bf16[40,128,128]{2,1,0:T(8,128)(2,1)} %bitcast.233, s32[1024]{0:T(1024)S(1)} %pad_clamp_fusion), kind=kCustom, calls=%fused_computation.1 | custom fusion | bytes 8913440 | tf_op jit(solution)/shard_map/gather | solution.py:37
  23.7 0.0 copy-start.2
  23.7 1.3 copy-done.2
  25.0 7.5 %gather_fusion = bf16[136,128,128]{2,1,0:T(8,128)(2,1)} fusion(bf16[40,128,128]{2,1,0:T(8,128)(2,1)S(1)} %bitcast.234, s32[1024]{0:T(1024)S(1)} %pad_clamp_fusion), kind=kCustom, calls=%fused_computation | custom fusion | bytes 8913440 | tf_op jit(solution)/shard_map/gather | solution.py:36
  32.5 0.0 copy-start.9
  32.6 0.0 copy-start.14
  32.6 0.0 slice-start.1
  32.6 0.8 copy-done.9
  33.4 1.7 select_reduce_fusion
  35.2 0.3 bitcast_reduce_fusion
  35.5 0.2 convolution_bitcast_fusion.2
  35.7 0.0 slice-start.2
  35.7 0.0 copy-start.8
  35.7 0.3 fusion.43
  36.1 0.1 broadcast_compare_fusion
  36.2 0.1 fusion.88
  36.4 0.0 slice-done.3
  36.4 0.0 copy-start.3
  36.4 1.3 select_reduce_fusion.1
  37.7 0.3 bitcast_reduce_fusion.1
  38.0 1.4 slice-done.2
  39.4 0.0 copy-start.4
  39.4 0.8 fusion.45
  40.1 0.0 copy-done.3
  40.1 1.6 convolution_convert_fusion
  41.8 0.0 reduce-scatter.5.cloned.1.call-update
  41.8 0.0 all-gather.2.cloned.1.call-start
  41.9 0.1 copy.38
  42.0 0.1 eq.56
  42.0 0.1 fusion.82
  42.8 0.1 reduce_window_sum.11
  42.8 0.2 select_reduce_fusion.3
  43.0 0.1 reduce_sum.82
  43.1 0.1 copy.39
  43.2 0.0 copy-done.16
  43.2 0.1 select_reduce_fusion.4
  43.4 24.8 %reduce-scatter.5.cloned.1.call-done = bf16[16,4096]{1,0:T(8,128)(2,1)} async-done(((bf16[64,4096]{1,0:T(8,128)(2,1)}), bf16[16,4096]{1,0:T(8,128)(2,1)}) %reduce-scatter.5.cloned.1.call-update) | async-done | bytes 131088 | tf_op jit(solution)/shard_map/reduce_scatter | solution.py:190
  68.1 1.1 fusion.53
  69.2 1.2 fusion.5
  70.4 0.2 copy.41
  70.6 15.7 %all_to_all.10 = bf16[8,1,6,4096]{3,2,1,0:T(8,128)(2,1)S(1)} all-to-all(bf16[8,1,6,4096]{3,2,1,0:T(8,128)(2,1)S(1)} %copy.41), channel_id=1, replica_groups=mesh['dp'=8,'expert'=8,'tensor'=4] {'expert'}, dimensions={0} | all-to-all | bytes 786432 | tf_op jit(solution)/shard_map/all_to_all | solution.py:116
  86.4 1.0 copy.42
  87.4 0.0 all-gather.2.cloned.1.call-update
  87.4 0.2 reduce-scatter.7.cloned.1.call-start
  87.6 117.5 %all-gather.2.cloned.1.call-done = bf16[256,1,6,4096]{3,0,2,1:T(8,128)(2,1)} async-done(((bf16[8,1,6,4096]{3,0,2,1:T(8,128)(2,1)}), bf16[256,1,6,4096]{3,0,2,1:T(8,128)(2,1)}) %all-gather.2.cloned.1.call-update) | async-done | bytes 12582928 | tf_op jit(solution)/shard_map/all_gather | solution.py:123
  205.1 7.5 %fusion.9 = f32[256,1,6,224]{0,3,2,1:T(8,128)S(1)} fusion(bf16[1,224,4096]{2,1,0:T(8,128)(2,1)} %param.31, bf16[256,1,6,4096]{3,0,2,1:T(8,128)(2,1)} %all-gather.2.cloned.1.call-done), kind=kOutput, calls=%fused_computation.15 | convolution fusion | flops 2818572288 | bytes 15794176 | tf_op jit(solution)/shard_map/qesd,efd->qesf/dot_general | solution.py:124
  212.6 19.3 %fusion.97 = bf16[32,8,6,4096]{3,1,0,2:T(8,128)(2,1)} fusion(bf16[1,224,4096]{2,1,0:T(8,128)(2,1)S(1)} %copy-done, bf16[1,224,4096]{2,1,0:T(8,128)(2,1)} %param.32, bf16[256,1,6,4096]{3,0,2,1:T(8,128)(2,1)} %all-gather.2.cloned.1.call-done, f32[256,1,6,224]{0,3,2,1:T(8,128)S(1)} %fusion.9), kind=kOutput, calls=%fused_computation.124 | convolution fusion | flops 5645500416 | bytes 30212096 | tf_op jit(solution)/shard_map/qesf,efd->qesd/dot_general | solution.py:132
  231.9 10.6 %copy.58 = bf16[32,8,6,4096]{3,1,2,0:T(8,128)(2,1)} copy(bf16[32,8,6,4096]{3,1,0,2:T(8,128)(2,1)} %fusion.97) | data formatting | bytes 25165824
  242.5 0.0 reduce-scatter.7.cloned.1.call-update
  242.6 0.0 copy-start.1
  242.6 230.3 %reduce-scatter.7.cloned.1.call-done = bf16[8,24576]{1,0:T(8,128)(2,1)} async-done(((bf16[256,24576]{1,0:T(8,128)(2,1)}), bf16[8,24576]{1,0:T(8,128)(2,1)}) %reduce-scatter.7.cloned.1.call-update) | async-done | bytes 393232
  472.9 1.2 copy.43
  474.1 18.4 %all_to_all.11 = bf16[8,1,6,4096]{3,2,1,0:T(8,128)(2,1)S(1)} all-to-all(bf16[8,1,6,4096]{3,2,1,0:T(8,128)(2,1)S(1)} %copy.43), channel_id=1, replica_groups=mesh['dp'=8,'expert'=8,'tensor'=4] {'expert'}, dimensions={0} | all-to-all | bytes 786432 | tf_op jit(solution)/shard_map/all_to_all | solution.py:139
  492.6 0.3 fusion.39
  492.9 0.7 fusion.56
  (49 shorter events, 0.3 us)
Async XLA Ops:
  6.5 206.1 %copy-start = (bf16[1,224,4096]{2,1,0:T(8,128)(2,1)S(1)}, bf16[1,224,4096]{2,1,0:T(8,128)(2,1)}, u32[]{:S(2)}) copy-start(bf16[1,224,4096]{2,1,0:T(8,128)(2,1)} %param.33) | copy-start | bytes 5505028
  6.5 61.6 %reduce-scatter.5.cloned.1.call-start = ((), (), s32[]{:S(2)}) async-start(), calls=%async_computation.4 | async-start | bytes 655360 | tf_op jit(solution)/shard_map/reduce_scatter | solution.py:190
  23.7 1.3 copy-start.2
  25.0 10.7 %slice-start = ((s8[4456448]{0:T(1024)(128)(4,1)}), s8[262144]{0:T(1024)(128)(4,1)S(1)}, s32[]{:S(2)}) async-start(s8[4456448]{0:T(1024)(128)(4,1)} %bitcast.229), calls=%async_computation.7 | async-start | bytes 524288
  32.5 0.8 copy-start.9
  32.5 0.8 copy-start.13
  32.6 2.6 copy-start.11
  32.6 2.9 copy-start.14
  32.6 3.1 slice-start.1
  33.4 2.7 copy-start.15
  33.4 2.8 copy-start.10
  33.4 3.0 slice-start.3
  35.7 3.6 slice-start.2
  35.7 3.6 copy-start.8
  36.4 3.8 copy-start.3
  39.3 2.5 copy-start.6
  39.3 3.8 copy-start.7
  39.3 3.8 copy-start.16
  39.4 28.8 %copy-start.4 = (bf16[16,4096]{1,0:T(8,128)(2,1)S(1)}, bf16[16,4096]{1,0:T(8,128)(2,1)}, u32[]{:S(2)}) copy-start(bf16[16,4096]{1,0:T(8,128)(2,1)} %param.17) | copy-start | bytes 393220
  41.8 163.3 %all-gather.2.cloned.1.call-start = ((), (), s32[]{:S(2)}) async-start(), calls=%async_computation.5 | async-start | bytes 12976128 | tf_op jit(solution)/shard_map/all_gather | solution.py:123
  87.4 385.5 %reduce-scatter.7.cloned.1.call-start = ((), (), s32[]{:S(2)}) async-start(), calls=%async_computation.6 | async-start | bytes 12976128
  242.5 250.0 %copy-start.12 = (f32[16,2]{0,1:T(2,128)S(1)}, f32[16,2]{0,1:T(2,128)}, u32[]{:S(2)}) copy-start(f32[16,2]{0,1:T(2,128)} %param.28) | copy-start | bytes 388
  242.5 250.4 %copy-start.5 = (bf16[16,4096]{1,0:T(8,128)(2,1)S(1)}, bf16[16,4096]{1,0:T(8,128)(2,1)}, u32[]{:S(2)}) copy-start(bf16[16,4096]{1,0:T(8,128)(2,1)} %reduce-scatter.5.cloned.1.call-done) | copy-start | bytes 393220
  242.6 251.1 %copy-start.1 = (bf16[1,224,4096]{2,1,0:T(8,128)(2,1)S(1)}, bf16[1,224,4096]{2,1,0:T(8,128)(2,1)}, u32[]{:S(2)}) copy-start(bf16[1,224,4096]{2,1,0:T(8,128)(2,1)} %param.33) | copy-start | bytes 5505028
Sparse Core Ops, SparseCore 0:
  41.9 26.1 reduce-scatter.4
  87.5 117.5 all-gather.1
  242.7 230.1 reduce-scatter.6
where the time goes:
time: 501 us; the launch traced here: 500 us
  waiting for transfers between devices  373 us (74%)
  local copies, waits for them, and re-layouts  36.9 us (7%)
  matrix products  35.9 us (7%)
  blocking collectives  34.2 us (7%)
  between operations  14.1 us (3%)
  other arithmetic  6.11 us (1%)
    unnamed x4, waiting for transfers between devices  230 us
    all_gather x1, waiting for transfers between devices, expert_pass(): row_piece = lax.all_gather(arrived, ('dp', 'tensor'), axis=0, tiled=True)  118 us
    reduce_scatter x1, waiting for transfers between devices, local(): lax.psum_scatter(jnp.dot(heads_out, attention_merge_matrix, preferred_ele...  24.8 us
    dot_general x1, matrix products, expert_pass(): jnp.einsum('qesf,efd->qesd', hidden, contract_matrices, preferred_element...  19.3 us
    all_to_all x1, blocking collectives, expert_pass(): lax.all_to_all(summed, 'expert', split_axis=0, concat_axis=0, tiled=True)  18.4 us
    all_to_all x1, blocking collectives, expert_pass(): lax.all_to_all(send.reshape(holders, local_count, slot_count, model_width...  15.7 us
    unnamed x42, local copies, waits for them, and re-layouts  12.9 us
  transfers between devices with their start and end apart: 3, of which 3 were waited for; matrix products, arithmetic and copies ran while one was open for 0% of the time, Pallas kernels for 0%

commit v1 on v0

--- a/solution.py
+++ b/solution.py
@@ -120,7 +120,11 @@
         concat_axis=0,
         tiled=True,
     )
-    row_piece = lax.all_gather(arrived, ("dp", "tensor"), axis=0, tiled=True)
+    size = lax.axis_size(("dp", "tensor"))
+    repeats = [size if d == 0 else 1 for d in range(arrived.ndim)]
+    row_piece = lax.all_to_all(
+        jnp.tile(arrived, repeats), ("dp", "tensor"), split_axis=0, concat_axis=0, tiled=True
+    )
     gate_part = jnp.einsum(
         "qesd,efd->qesf", row_piece, gating_matrices, preferred_element_type=jnp.float32
     )

time: 501 us -> 771 us (1.54)
  blocking collectives: 34.2 us -> 405 us
  waiting for transfers between devices: 373 us -> 256 us
  matrix products: 35.9 us -> 46.4 us
    all_to_all x0 -> x1, blocking collectives: none -> 371 us  [expert_pass(): lax.all_to_all(jnp.tile(arrived, repeats), ('dp', 'tensor'), split_axis=0...]
    all_gather x1 -> x0, waiting for transfers between devices: 118 us -> none  [expert_pass(): row_piece = lax.all_gather(arrived, ('dp', 'tensor'), axis=0, tiled=True)]
    dot_general x1, matrix products: 19.3 us -> 29.2 us  [expert_pass(): jnp.einsum('qesf,efd->qesd', hidden, contract_matrices, preferred_element...]
    unnamed x42 -> x44, local copies, waits for them, and re-layouts: 12.9 us -> 18.7 us
    unnamed x4 -> x3, waiting for transfers between devices: 230 us -> 231 us
  transfers between devices with their start and end apart: 3 -> 2, of which waited for: 3 -> 2; matrix products, arithmetic and copies ran while one was open for 0% -> 0% of each run, Pallas kernels for 0% -> 0%
where the time goes in v1:
time: 771 us
  blocking collectives  405 us (53%)
  waiting for transfers between devices  256 us (33%)
  matrix products  46.4 us (6%)
  local copies, waits for them, and re-layouts  43.6 us (6%)
  between operations  14.4 us (2%)
    all_to_all x1, blocking collectives, expert_pass(): lax.all_to_all(jnp.tile(arrived, repeats), ('dp', 'tensor'), split_axis=0...  371 us
    unnamed x3, waiting for transfers between devices  231 us
    dot_general x1, matrix products, expert_pass(): jnp.einsum('qesf,efd->qesd', hidden, contract_matrices, preferred_element...  29.2 us
    reduce_scatter x1, waiting for transfers between devices, local(): lax.psum_scatter(jnp.dot(heads_out, attention_merge_matrix, preferred_ele...  24.8 us
    unnamed x44, local copies, waits for them, and re-layouts  18.7 us
    all_to_all x1, blocking collectives, expert_pass(): lax.all_to_all(summed, 'expert', split_axis=0, concat_axis=0, tiled=True)  18.2 us
    all_to_all x1, blocking collectives, expert_pass(): lax.all_to_all(send.reshape(holders, local_count, slot_count, model_width...  15.7 us
  transfers between devices with their start and end apart: 2, of which 2 were waited for; matrix products, arithmetic and copies ran while one was open for 0% of the time, Pallas kernels for 0%

profile of v1, /device:TPU:1, one launch (start us, length us, event | category | flops | bytes accessed | tf_op | source)
XLA Modules:
  0.0 770.9 jit_solution(8668761987620978146)
XLA Ops:
  6.5 0.0 copy-start
  6.6 0.9 slice.44
  7.4 1.2 slice.49
  8.7 1.2 broadcast_compare_fusion.1
  9.8 0.7 compare_select_fusion
  10.5 1.3 slice_bitcast_fusion.5
  11.8 0.1 copy.32
  11.9 0.1 reshape.338
  12.0 1.3 slice_convert_fusion
  13.3 1.6 select_reduce_fusion.2
  14.8 8.8 %gather_fusion.1 = bf16[136,128,128]{2,1,0:T(8,128)(2,1)} fusion(bf16[40,128,128]{2,1,0:T(8,128)(2,1)} %bitcast.236, s32[1024]{0:T(1024)S(1)} %pad_clamp_fusion), kind=kCustom, calls=%fused_computation.1 | custom fusion | bytes 8913440 | tf_op jit(solution)/shard_map/gather | solution.py:37
  23.7 0.0 copy-start.2
  23.7 1.3 copy-done.2
  25.0 7.5 gather_fusion
  32.5 0.0 copy-start.9
  32.6 0.0 copy-start.14
  32.6 0.0 slice-start.1
  32.6 0.8 copy-done.9
  33.4 1.7 select_reduce_fusion
  35.2 0.3 bitcast_reduce_fusion
  35.5 0.2 convolution_bitcast_fusion.2
  35.7 0.0 slice-start.2
  35.7 0.0 copy-start.8
  35.7 0.3 fusion.41
  36.1 0.1 broadcast_compare_fusion
  36.2 0.1 fusion.90
  36.4 0.0 slice-done.3
  36.4 0.0 copy-start.3
  36.4 1.3 select_reduce_fusion.1
  37.7 0.3 bitcast_reduce_fusion.1
  38.0 1.4 slice-done.2
  39.4 0.0 copy-start.4
  39.4 0.8 fusion.43
  40.1 0.0 copy-done.3
  40.1 1.6 convolution_convert_fusion
  41.8 0.0 reduce-scatter.5.cloned.1.call-update
  41.8 0.0 reduce-scatter.7.cloned.1.call-start
  41.9 0.1 copy.38
  42.0 0.1 eq.56
  42.0 0.1 fusion.84
  42.8 0.1 reduce_window_sum.11
  42.8 0.2 select_reduce_fusion.3
  43.0 0.1 reduce_sum.82
  43.1 0.1 copy.39
  43.2 0.0 copy-done.17
  43.2 0.1 select_reduce_fusion.4
  43.4 24.8 %reduce-scatter.5.cloned.1.call-done = bf16[16,4096]{1,0:T(8,128)(2,1)} async-done(((bf16[64,4096]{1,0:T(8,128)(2,1)}), bf16[16,4096]{1,0:T(8,128)(2,1)}) %reduce-scatter.5.cloned.1.call-update) | async-done | bytes 131088 | tf_op jit(solution)/shard_map/reduce_scatter | solution.py:194
  68.1 1.1 fusion.55
  69.2 1.2 fusion.7
  70.4 0.2 copy.41
  70.6 15.7 %all_to_all.15 = bf16[8,1,6,4096]{3,2,1,0:T(8,128)(2,1)S(1)} all-to-all(bf16[8,1,6,4096]{3,2,1,0:T(8,128)(2,1)S(1)} %copy.41), channel_id=1, replica_groups=mesh['dp'=8,'expert'=8,'tensor'=4] {'expert'}, dimensions={0} | all-to-all | bytes 786432 | tf_op jit(solution)/shard_map/all_to_all | solution.py:116
  86.4 1.9 tile.12
  88.3 0.0 copy-start.16
  88.3 370.7 %all_to_all.16 = bf16[256,1,6,4096]{3,2,1,0:T(8,128)(2,1)S(1)} all-to-all(bf16[256,1,6,4096]{3,2,1,0:T(8,128)(2,1)S(1)} %bitcast.230), channel_id=1, replica_groups=mesh['dp'=8,'expert'=8,'tensor'=4] {'dp','tensor'}, dimensions={0} | all-to-all | bytes 25165824 | tf_op jit(solution)/shard_map/all_to_all | solution.py:125
  459.1 5.7 copy-done.1
  464.8 8.0 %fusion.11 = f32[256,1,6,224]{0,3,2,1:T(8,128)S(1)} fusion(bf16[1,224,4096]{2,1,0:T(8,128)(2,1)S(1)} %copy-done.16, bf16[256,1,6,4096]{3,2,1,0:T(8,128)(2,1)S(1)} %all_to_all.16), kind=kOutput, calls=%fused_computation.17 | convolution fusion | flops 2818572288 | bytes 15794176 | tf_op jit(solution)/shard_map/qesd,efd->qesf/dot_general | solution.py:128
  472.9 29.2 %fusion.99 = bf16[32,8,6,4096]{3,1,0,2:T(8,128)(2,1)} fusion(bf16[1,224,4096]{2,1,0:T(8,128)(2,1)S(1)} %copy-done, bf16[1,224,4096]{2,1,0:T(8,128)(2,1)} %param.32, bf16[256,1,6,4096]{3,2,1,0:T(8,128)(2,1)} %copy-done.1, f32[256,1,6,224]{0,3,2,1:T(8,128)S(1)} %fusion.11), kind=kOutput, calls=%fused_computation.126 | convolution fusion | flops 5645500416 | bytes 30212096 | tf_op jit(solution)/shard_map/qesf,efd->qesd/dot_general | solution.py:136
  502.1 10.6 %copy.58 = bf16[32,8,6,4096]{3,1,2,0:T(8,128)(2,1)} copy(bf16[32,8,6,4096]{3,1,0,2:T(8,128)(2,1)} %fusion.99) | data formatting | bytes 25165824
  512.7 0.0 reduce-scatter.7.cloned.1.call-update
  512.7 230.8 %reduce-scatter.7.cloned.1.call-done = bf16[8,24576]{1,0:T(8,128)(2,1)} async-done(((bf16[256,24576]{1,0:T(8,128)(2,1)}), bf16[8,24576]{1,0:T(8,128)(2,1)}) %reduce-scatter.7.cloned.1.call-update) | async-done | bytes 393232
  743.5 1.2 copy.43
  744.7 18.2 %all_to_all.17 = bf16[8,1,6,4096]{3,2,1,0:T(8,128)(2,1)S(1)} all-to-all(bf16[8,1,6,4096]{3,2,1,0:T(8,128)(2,1)S(1)} %copy.43), channel_id=1, replica_groups=mesh['dp'=8,'expert'=8,'tensor'=4] {'expert'}, dimensions={0} | all-to-all | bytes 786432 | tf_op jit(solution)/shard_map/all_to_all | solution.py:143
  763.0 0.3 fusion.37
  763.3 0.7 fusion.58
  (49 shorter events, 0.3 us)
Async XLA Ops:
  6.5 466.3 %copy-start = (bf16[1,224,4096]{2,1,0:T(8,128)(2,1)S(1)}, bf16[1,224,4096]{2,1,0:T(8,128)(2,1)}, u32[]{:S(2)}) copy-start(bf16[1,224,4096]{2,1,0:T(8,128)(2,1)} %param.33) | copy-start | bytes 5505028
  6.5 61.6 %reduce-scatter.5.cloned.1.call-start = ((), (), s32[]{:S(2)}) async-start(), calls=%async_computation.5 | async-start | bytes 655360 | tf_op jit(solution)/shard_map/reduce_scatter | solution.py:194
  23.7 1.3 copy-start.2
  25.0 10.7 %slice-start = ((s8[4456448]{0:T(1024)(128)(4,1)}), s8[262144]{0:T(1024)(128)(4,1)S(1)}, s32[]{:S(2)}) async-start(s8[4456448]{0:T(1024)(128)(4,1)} %bitcast.232), calls=%async_computation.7 | async-start | bytes 524288
  32.5 0.8 copy-start.9
  32.5 0.8 copy-start.13
  32.6 2.6 copy-start.11
  32.6 2.9 copy-start.14
  32.6 3.1 slice-start.1
  33.4 2.7 copy-start.15
  33.4 2.8 copy-start.10
  33.4 3.0 slice-start.3
  35.7 3.6 slice-start.2
  35.7 3.6 copy-start.8
  36.4 3.8 copy-start.3
  39.3 2.5 copy-start.6
  39.3 3.8 copy-start.7
  39.3 3.8 copy-start.17
  39.4 28.8 %copy-start.4 = (bf16[16,4096]{1,0:T(8,128)(2,1)S(1)}, bf16[16,4096]{1,0:T(8,128)(2,1)}, u32[]{:S(2)}) copy-start(bf16[16,4096]{1,0:T(8,128)(2,1)} %param.17) | copy-start | bytes 393220
  41.8 701.7 %reduce-scatter.7.cloned.1.call-start = ((), (), s32[]{:S(2)}) async-start(), calls=%async_computation.6 | async-start | bytes 12976128
  88.3 376.5 %copy-start.16 = (bf16[1,224,4096]{2,1,0:T(8,128)(2,1)S(1)}, bf16[1,224,4096]{2,1,0:T(8,128)(2,1)}, u32[]{:S(2)}) copy-start(bf16[1,224,4096]{2,1,0:T(8,128)(2,1)} %param.31) | copy-start | bytes 5505028
  459.1 5.7 copy-start.1
  512.7 250.3 %copy-start.12 = (f32[16,2]{0,1:T(2,128)S(1)}, f32[16,2]{0,1:T(2,128)}, u32[]{:S(2)}) copy-start(f32[16,2]{0,1:T(2,128)} %param.28) | copy-start | bytes 388
  512.7 250.6 %copy-start.5 = (bf16[16,4096]{1,0:T(8,128)(2,1)S(1)}, bf16[16,4096]{1,0:T(8,128)(2,1)}, u32[]{:S(2)}) copy-start(bf16[16,4096]{1,0:T(8,128)(2,1)} %reduce-scatter.5.cloned.1.call-done) | copy-start | bytes 393220
Sparse Core Ops, SparseCore 0:
  41.9 26.1 reduce-scatter.4
  512.9 230.6 reduce-scatter.6
